TPU v7x, 32 devices: a whole 2x2x4 slice. The times are simulated.
32 devices in a mesh: groups: 2 (over y), row: 4 (over z), col: 2 (over x), aux: 2 (over core).
Axes of the slice: x: 2, y: 2, z: 4, core: 2. Of those that a mesh axis runs over, the one named last changes fastest.
Arguments:
- amplitudes: bfloat16 [32768, 16384], P(('groups', 'row'), ('col', 'aux')), parts along dimension 0, may hold values from -6 to 6, as said below
- b_factors: bfloat16 [32768, 512], P(('groups', 'row'), ('col', 'aux')), parts along dimension 0, may hold values from -0.25 to 0.25
- fock_blocks: bfloat16 [32768, 256], P(('groups', 'row')), parts along dimension 0, may hold values from -0.375 to 0.375
- occ_index: int32 [32768], P('groups'), parts along dimension 0, may hold values from 0 to 63, as said below
- virt_index: int32 [32768], P('groups'), parts along dimension 0, may hold values from 0 to 255, as said below
- eps_occ: float32 [128], P('groups'), parts along dimension 0, may hold values from -3 to -0.5
- eps_virt: float32 [512], P('groups'), parts along dimension 0, may hold values from 0.5 to 3
Outputs:
- t_next: bfloat16 [32768, 16384], P(('groups', 'row'), ('col', 'aux')), parts along dimension 0
There are 2 independent parts, one for each index of `groups`. A program takes and returns all parts, laid end to end along the dimension named above; each array names one. Nothing has to cross between parts.
Inputs may be any that keep to these rules, and one draw needn't show every extreme that they name: amplitudes is symmetric: amplitudes[p, q] == amplitudes[q, p]. `occ_index`: pairs are occupied-major: all pairs of diagonal block k (p // 256 == k) share one occupied orbital, and distinct blocks have distinct ones. `virt_index`: within each diagonal block the 256 pairs have distinct virtual orbitals, in the same order for every block.
All inputs are finite; a program needn't handle non-finite values.
Results may differ from a plain program's by a relative error of at most 0.0023.
Values may be sent and summed in bfloat16 or wider, within the bound.
A program may use at most 512 MiB of HBM per device.

v0:
```python
import jax
import jax.numpy as jnp
from jax import lax
from jax.sharding import PartitionSpec as P


def spread(shard, axis, root):
    mine = lax.axis_index(axis) == root
    return lax.psum(jnp.where(mine, shard, jnp.zeros_like(shard)), axis)


def pair_energy(occ_part, virt_part, eps_occ, eps_virt):
    virt_hit = virt_part[:, None] == jnp.arange(eps_virt.shape[0], dtype=jnp.int32)[None, :]
    occ_hit = occ_part[:, None] == jnp.arange(eps_occ.shape[0], dtype=jnp.int32)[None, :]
    upper = jnp.sum(jnp.where(virt_hit, eps_virt[None, :], 0.0), axis=1)
    lower = jnp.sum(jnp.where(occ_hit, eps_occ[None, :], 0.0), axis=1)
    return upper - lower


def body(amplitudes, b_factors, fock_blocks, occ_index, virt_index, eps_occ, eps_virt):
    rows_blk = amplitudes.shape[0]
    aux_width = b_factors.shape[1] * lax.axis_size(("col", "aux"))
    virt_count = eps_virt.shape[0]
    b_rows = lax.all_gather(b_factors, ("col", "aux"), axis=1, tiled=True)
    g_part = lax.psum_scatter(
        lax.dot_general(
            amplitudes, b_rows, (((0,), (0,)), ((), ())), preferred_element_type=jnp.float32
        ),
        "row",
        scatter_dimension=0,
        tiled=True,
    )
    g_slice = g_part.astype(jnp.bfloat16)
    g_cols = lax.all_gather(g_slice, "row", axis=0, tiled=True)
    packed = jnp.concatenate([b_rows, fock_blocks], axis=1)
    mirror = spread(packed, "row", lax.axis_index(("col", "aux")))
    b_cols = mirror[:, :aux_width]
    fock_cols = mirror[:, aux_width:]
    g_rows = spread(g_cols, ("col", "aux"), lax.axis_index("row"))
    contract = (((1,), (1,)), ((), ()))
    residual = lax.dot_general(g_rows, b_cols, contract, preferred_element_type=jnp.float32)
    residual = residual + lax.dot_general(
        b_rows, g_cols, contract, preferred_element_type=jnp.float32
    )
    blocks = rows_blk // virt_count
    tshaped = amplitudes.reshape(rows_blk, blocks, virt_count)
    right = jnp.einsum(
        "xkd,kde->xke",
        tshaped,
        fock_cols.reshape(blocks, virt_count, virt_count),
        preferred_element_type=jnp.float32,
    )
    left = jnp.einsum(
        "kcr,kcy->kry",
        fock_blocks.reshape(blocks, virt_count, virt_count),
        amplitudes.reshape(blocks, virt_count, rows_blk),
        preferred_element_type=jnp.float32,
    )
    residual = residual + right.reshape(rows_blk, rows_blk) + left.reshape(rows_blk, rows_blk)
    first_start = lax.axis_index("row") * rows_blk
    second_start = lax.axis_index(("col", "aux")) * rows_blk
    energy_first = pair_energy(
        lax.dynamic_slice_in_dim(occ_index, first_start, rows_blk),
        lax.dynamic_slice_in_dim(virt_index, first_start, rows_blk),
        eps_occ,
        eps_virt,
    )
    energy_second = pair_energy(
        lax.dynamic_slice_in_dim(occ_index, second_start, rows_blk),
        lax.dynamic_slice_in_dim(virt_index, second_start, rows_blk),
        eps_occ,
        eps_virt,
    )
    delta = energy_first[:, None] + energy_second[None, :]
    return (amplitudes.astype(jnp.float32) - residual / delta).astype(jnp.bfloat16)


def solution(mesh):
    in_specs = (
        P(("groups", "row"), ("col", "aux")),
        P(("groups", "row"), ("col", "aux")),
        P(("groups", "row"), None),
        P("groups"),
        P("groups"),
        P("groups"),
        P("groups"),
    )
    out_specs = P(("groups", "row"), ("col", "aux"))
    return jax.shard_map(body, mesh=mesh, in_specs=in_specs, out_specs=out_specs, check_vma=False)
```

profile of v0, /device:TPU:24, one launch (start us, length us, event | category | flops | bytes accessed | tf_op | source)
XLA Modules:
  0.0 759.2 jit_solution(16009401869180212808)
XLA Ops:
  6.5 0.0 all-gather.3.cloned.1.call-start
  6.5 0.7 all-gather.3.cloned.1.call-update
  7.3 0.0 reduce-scatter.2.cloned.1.call-start
  7.3 37.6 %all-gather.3.cloned.1.call-done = bf16[4096,512]{1,0:T(8,128)(2,1)} async-done(((bf16[4096,128]{1,0:T(8,128)(2,1)}), bf16[4096,512]{1,0:T(8,128)(2,1)}) %all-gather.3.cloned.1.call-update) | async-done | bytes 4194320 | tf_op jit(solution)/shard_map/all_gather | solution.py:24
  44.9 25.5 %fusion.11 = f32[4096,512]{1,0:T(8,128)} fusion(bf16[4096,4096]{1,0:T(8,128)(2,1)} %param.7, bf16[4096,512]{1,0:T(8,128)(2,1)} %all-gather.3.cloned.1.call-done), kind=kOutput, calls=%fused_computation.23 | convolution fusion | flops 17179869184 | bytes 46137344 | tf_op jit(solution)/shard_map/dot_general | solution.py:26
  70.5 0.0 copy-start
  70.5 0.0 reduce-scatter.2.cloned.1.call-update
  70.5 0.0 all-reduce.5.cloned.1.call-start
  70.5 1.5 copy-done
  72.0 5.8 maximum_select_fusion
  77.9 0.0 all-reduce.5.cloned.1.call-update
  77.9 0.0 all-gather.5.cloned.1.call-start
  78.0 136.6 %reduce-scatter.2.cloned.1.call-done = f32[1024,512]{1,0:T(8,128)} async-done(((f32[4096,512]{1,0:T(8,128)}), f32[1024,512]{1,0:T(8,128)}) %reduce-scatter.2.cloned.1.call-update) | async-done | bytes 2097168 | tf_op jit(solution)/shard_map/reduce_scatter | solution.py:25
  214.6 2.7 convert_element_type.10
  217.3 0.0 all-gather.5.cloned.1.call-update
  217.3 0.2 all-reduce.3.cloned.1.call-start
  217.5 0.0 copy-done.1
  217.5 0.0 copy-done.2
  217.6 0.0 copy-done.4
  217.6 0.4 select_reduce_fusion.3
  218.0 0.0 copy-done.3
  218.0 2.6 select_reduce_fusion.1
  220.6 33.6 %fusion.12 = f32[16,256,4096]{2,1,0:T(8,128)} fusion(bf16[16,256,256]{2,1,0:T(8,128)(2,1)S(1)} %bitcast.34, bf16[16,256,4096]{2,1,0:T(8,128)(2,1)} %bitcast.32), kind=kOutput, calls=%fused_computation.24 | convolution fusion | flops 8589934592 | bytes 102760448 | tf_op jit(solution)/shard_map/kcr,kcy->kry/dot_general | solution.py:53
  254.2 184.6 %all-reduce.5.cloned.1.call-done = bf16[4096,768]{1,0:T(8,128)(2,1)} async-done(((bf16[4096,768]{1,0:T(8,128)(2,1)}), bf16[4096,768]{1,0:T(8,128)(2,1)}) %all-reduce.5.cloned.1.call-update) | async-done | bytes 6291472 | tf_op jit(solution)/shard_map/psum | solution.py:9
  438.8 80.7 %all-gather.5.cloned.1.call-done = bf16[4096,512]{1,0:T(8,128)(2,1)} async-done(((bf16[1024,512]{1,0:T(8,128)(2,1)}), bf16[4096,512]{1,0:T(8,128)(2,1)}) %all-gather.5.cloned.1.call-update) | async-done | bytes 4194320 | tf_op jit(solution)/shard_map/all_gather | solution.py:34
  519.5 2.3 broadcast_select_fusion
  521.8 0.0 all-reduce.3.cloned.1.call-update
  521.9 0.0 slice-done
  521.9 48.9 %fusion.4 = f32[16,256,4096]{2,1,0:T(8,128)} fusion(bf16[16,256,256]{2,1,0:T(8,128)(2,1)S(1)} %bitcast.35, bf16[512,16,8,256]{3,2,1,0:T(8,128)(2,1)} %bitcast.33), kind=kOutput, calls=%fused_computation.6 | convolution fusion | flops 8589934592 | bytes 102760448 | tf_op jit(solution)/shard_map/xkd,kde->xke/dot_general | solution.py:47
  570.8 66.1 %copy.25 = f32[4096,4096]{1,0:T(8,128)} copy(f32[4096,4096]{0,1:T(8,128)} %bitcast.3) | data formatting | bytes 134217728 | tf_op jit(solution)/shard_map/reshape | solution.py:59
  636.9 30.0 %fusion.7 = f32[4096,4096]{1,0:T(8,128)} fusion(bf16[4096,512]{1,0:T(8,128)(2,1)} %all-reduce.3.cloned.1.call-done, bf16[4096,768]{1,0:T(8,128)(2,1)} %all-reduce.5.cloned.1.call-done), kind=kOutput, calls=%fused_computation.10 | convolution fusion | flops 17179869184 | bytes 75497472 | tf_op jit(solution)/shard_map/dot_general | solution.py:41
  666.9 85.7 %fusion.2 = bf16[4096,4096]{1,0:T(8,128)(2,1)} fusion(f32[16,256,4096]{2,1,0:T(8,128)} %fusion.12, f32[4096,4096]{1,0:T(8,128)} %copy.25, f32[4096,4096]{1,0:T(8,128)} %fusion.7, bf16[4096,4096]{1,0:T(8,128)(2,1)} %param.7, bf16[4096,512]{1,0:T(8,128)(2,1)} %all-gather.5.cloned.1.call-done, bf16[4096,512]{1,0:T(8,128)(2,1)} %all-gather.3.cloned.1.call-done, ...), kind=kOutput, calls=%fused_computation.3 | convolution fusion | flops 17314086912 | bytes 276856832 | tf_op jit(solution)/shard_map/dot_general | solution.py:42
  (9 shorter events, 0.0 us)
Async XLA Ops:
  6.5 38.4 %all-gather.3.cloned.1.call-start = ((), (), s32[]{:S(2)}) async-start(), calls=%async_computation.1 | async-start | bytes 5242880 | tf_op jit(solution)/shard_map/all_gather | solution.py:24
  7.3 207.3 %reduce-scatter.2.cloned.1.call-start = ((), (), s32[]{:S(2)}) async-start(), calls=%async_computation.2 | async-start | bytes 10485760 | tf_op jit(solution)/shard_map/reduce_scatter | solution.py:25
  70.5 1.6 copy-start
  70.5 368.3 %all-reduce.5.cloned.1.call-start = ((), (), s32[]{:S(2)}) async-start(), calls=%async_computation.5 | async-start | bytes 12582912 | tf_op jit(solution)/shard_map/psum | solution.py:9
  77.9 139.7 %copy-start.1 = (s32[16384]{0:T(1024)S(1)}, s32[16384]{0:T(1024)}, u32[]{:S(2)}) copy-start(s32[16384]{0:T(1024)} %param.10) | copy-start | bytes 196612
  77.9 139.7 %copy-start.2 = (s32[16384]{0:T(1024)S(1)}, s32[16384]{0:T(1024)}, u32[]{:S(2)}) copy-start(s32[16384]{0:T(1024)} %param.11) | copy-start | bytes 196612
  77.9 139.7 %copy-start.4 = (f32[64]{0:T(128)S(1)}, f32[64]{0:T(128)}, u32[]{:S(2)}) copy-start(f32[64]{0:T(128)} %param.12) | copy-start | bytes 772
  77.9 140.1 %copy-start.3 = (f32[256]{0:T(256)S(1)}, f32[256]{0:T(256)}, u32[]{:S(2)}) copy-start(f32[256]{0:T(256)} %param.13) | copy-start | bytes 3076
  77.9 441.6 %all-gather.5.cloned.1.call-start = ((), (), s32[]{:S(2)}) async-start(), calls=%async_computation.3 | async-start | bytes 5242880 | tf_op jit(solution)/shard_map/all_gather | solution.py:34
  217.3 419.6 %all-reduce.3.cloned.1.call-start = ((), (), s32[]{:S(2)}) async-start(), calls=%async_computation.4 | async-start | bytes 8388608 | tf_op jit(solution)/shard_map/psum | solution.py:9
  438.8 83.1 %slice-start = ((bf16[4096,768]{1,0:T(8,128)(2,1)}), bf16[4096,256]{1,0:T(8,128)(2,1)S(1)}, s32[]{:S(2)}) async-start(bf16[4096,768]{1,0:T(8,128)(2,1)} %all-reduce.5.cloned.1.call-done), calls=%async_computation.6 | async-start | bytes 4194304 | tf_op jit(solution)/shard_map/slice | solution.py:38
Sparse Core Ops, SparseCore 0:
  8.9 35.9 all-gather.2
  70.6 143.9 reduce-scatter.1
  216.9 221.7 all-reduce.4
  440.2 79.2 all-gather.4
  522.0 88.9 all-reduce.2
where the time goes:
time: 767 us; the launch traced here: 759 us
  waiting for transfers between devices  440 us (57%)
  matrix products  224 us (29%)
  local copies, waits for them, and re-layouts  67.7 us (9%)
  other arithmetic  13.8 us (2%)
  between operations  13.2 us (2%)
    psum x2, waiting for transfers between devices, spread(): return lax.psum(jnp.where(mine, shard, jnp.zeros_like(shard)), axis)  185 us
    reduce_scatter x1, waiting for transfers between devices, body(): lax.psum_scatter(lax.dot_general(amplitudes, b_rows, (((0,), (0,)), ((),...  137 us
    dot_general x1, matrix products, body(): lax.dot_general(b_rows, g_cols, contract, preferred_element_type=jnp.floa...  85.7 us
    all_gather x1, waiting for transfers between devices, body(): g_cols = lax.all_gather(g_slice, 'row', axis=0, tiled=True)  80.7 us
    reshape x1, local copies, waits for them, and re-layouts, body(): right.reshape(rows_blk, rows_blk)  66.1 us
    dot_general x1, matrix products, body(): jnp.einsum('xkd,kde->xke', tshaped, fock_cols.reshape(blocks, virt_count,...  48.9 us
    all_gather x1, waiting for transfers between devices, body(): b_rows = lax.all_gather(b_factors, ('col', 'aux'), axis=1, tiled=True)  37.6 us
    dot_general x1, matrix products, body(): jnp.einsum('kcr,kcy->kry', fock_blocks.reshape(blocks, virt_count, virt_c...  33.6 us
  transfers between devices with their start and end apart: 5, of which 4 were waited for; matrix products, arithmetic and copies ran while one was open for 21% of the time, Pallas kernels for 0%

commit v1 on v0

v1 whole, which is shorter than its diff:
```python
import functools

import jax
import jax.numpy as jnp
from jax import lax
from jax.experimental import pallas as pl
from jax.experimental.pallas import tpu as pltpu
from jax.sharding import PartitionSpec as P

MESH = pl.DeviceIdType.MESH
LANES = 128
ROW_TILE = 512
COL_TILE = 512
VMEM_BYTES = 60 * 1024 * 1024


def pair_energy(occ_part, virt_part, eps_occ, eps_virt):
    virt_hit = virt_part[:, None] == jnp.arange(eps_virt.shape[0], dtype=jnp.int32)[None, :]
    occ_hit = occ_part[:, None] == jnp.arange(eps_occ.shape[0], dtype=jnp.int32)[None, :]
    upper = jnp.sum(jnp.where(virt_hit, eps_virt[None, :], 0.0), axis=1)
    lower = jnp.sum(jnp.where(occ_hit, eps_occ[None, :], 0.0), axis=1)
    return upper - lower


def slab(ref, index, width, start, size):
    if width % LANES == 0:
        return ref.at[pl.ds(start, size), pl.ds(pl.multiple_of(index * width, LANES), width)]
    return ref.at[index, pl.ds(start, size)]


def slab_shape(count, rows, width):
    return (rows, count * width) if width % LANES == 0 else (count, rows, width)


def whole(array):
    if array.ndim == 2:
        return array
    count, rows, width = array.shape
    return array.transpose(1, 0, 2).reshape(rows, count * width)


def meet(row, col, aux, rows, cols, auxs):
    barrier = pltpu.get_barrier_semaphore()

    def greet(device):
        pl.semaphore_signal(barrier, inc=1, device_id=device, device_id_type=MESH)

    @pl.when(row > 0)
    def _():
        greet({"row": row - 1})

    @pl.when(row < rows - 1)
    def _():
        greet({"row": row + 1})

    for step in range(1, cols * auxs):
        other = lax.rem(col * auxs + aux + step, cols * auxs)
        greet({"col": other // auxs, "aux": lax.rem(other, auxs)})
    above = jnp.where(row > 0, 1, 0)
    below = jnp.where(row < rows - 1, 1, 0)
    pl.semaphore_wait(barrier, cols * auxs - 1 + above + below)


def exchange_kernel(
    rows, cols, auxs, pieces, loc, along, mine, other,
    zsend, zrecv, csend, crecv, rsend, rrecv, lsem,
):
    row, col, aux = lax.axis_index("row"), lax.axis_index("col"), lax.axis_index("aux")
    count = cols * auxs
    me = col * auxs + aux
    height, width = loc.shape
    size = height // pieces
    meet(row, col, aux, rows, cols, auxs)

    def held(k, p, own):
        return loc.at[pl.ds(p * size, size)] if own else along.at[k, pl.ds(p * size, size)]

    def z_copy(k, p, step, own=False):
        return pltpu.make_async_remote_copy(
            src_ref=held(k, p, own),
            dst_ref=along.at[k, pl.ds(p * size, size)],
            send_sem=zsend.at[(1 - step) // 2, k, p],
            recv_sem=zrecv.at[k, p],
            device_id={"row": row + step},
            device_id_type=MESH,
        )

    def c_copy(k, p, slot, own=False):
        return pltpu.make_async_remote_copy(
            src_ref=held(k, p, own),
            dst_ref=slab(other, slot, width, p * size, size),
            send_sem=csend.at[k, p],
            recv_sem=crecv.at[slot, p],
            device_id={"col": k // auxs, "aux": lax.rem(k, auxs)},
            device_id_type=MESH,
        )

    def c_local(k, p, own=False):
        return pltpu.make_async_copy(
            held(k, p, own), slab(other, me, width, p * size, size), lsem.at[1 + p]
        )

    def dispatch(k, p, own=False):
        @pl.when(k != me)
        def _():
            c_copy(k, p, me, own).start()

        @pl.when(k == me)
        def _():
            c_local(k, p, own).start()

    def r_copy(index, to_col, to_aux, hop, own):
        return pltpu.make_async_remote_copy(
            src_ref=loc if own else slab(mine, index, width, 0, height),
            dst_ref=slab(mine, index, width, 0, height),
            send_sem=rsend.at[hop],
            recv_sem=rrecv.at[index],
            device_id={"col": to_col, "aux": to_aux},
            device_id_type=MESH,
        )

    def r_sends():
        first, second = [], []
        for step in range(1, cols):
            first.append(r_copy(me, lax.rem(col + step, cols), aux, step - 1, True))
        hop = cols - 1
        for step in range(cols):
            from_col = lax.rem(col + step, cols)
            for turn in range(1, auxs):
                second.append((
                    from_col * auxs + aux,
                    r_copy(from_col * auxs + aux, col, lax.rem(aux + turn, auxs), hop, step == 0),
                ))
                hop += 1
        return first, second

    first, second = r_sends()
    for copy in first:
        copy.start()
    for _, copy in second[: auxs - 1]:
        copy.start()
    for p in range(pieces):
        @pl.when(row < rows - 1)
        def _(p=p):
            z_copy(row, p, 1, True).start()

        @pl.when(row > 0)
        def _(p=p):
            z_copy(row, p, -1, True).start()

        dispatch(row, p, True)
    local = pltpu.make_async_copy(loc, slab(mine, me, width, 0, height), lsem.at[0])
    local.start()

    for s in range(1, rows):
        for p in range(pieces):
            @pl.when(row - s >= 0)
            def _(s=s, p=p):
                k = row - s
                z_copy(k, p, 1).wait_recv()

                @pl.when(row < rows - 1)
                def _():
                    z_copy(k, p, 1).start()

                dispatch(k, p)

            @pl.when(row + s < rows)
            def _(s=s, p=p):
                k = row + s
                z_copy(k, p, -1).wait_recv()

                @pl.when(row > 0)
                def _():
                    z_copy(k, p, -1).start()

                dispatch(k, p)
        if s == 1:
            for index, copy in second[auxs - 1:]:
                r_copy(index, col, aux, 0, False).wait_recv()
                copy.start()

    for step in range(cols):
        from_col = lax.rem(col + step, cols)
        for turn in range(1, auxs):
            index = from_col * auxs + lax.rem(aux + turn, auxs)
            r_copy(index, col, aux, 0, False).wait_recv()
    for copy in first:
        copy.wait_send()
    for _, copy in second:
        copy.wait_send()
    local.wait()
    for step in range(1, count):
        index = lax.rem(me + step, count)
        for p in range(pieces):
            c_copy(me, p, index).wait_recv()
    for k in range(rows):
        for p in range(pieces):
            @pl.when(k != me)
            def _(k=k, p=p):
                c_copy(k, p, me).wait_send()

            @pl.when(k == me)
            def _(k=k, p=p):
                c_local(k, p).wait()

            @pl.when((row < rows - 1) & (row >= k))
            def _(k=k, p=p):
                z_copy(k, p, 1).wait_send()

            @pl.when((row > 0) & (row <= k))
            def _(k=k, p=p):
                z_copy(k, p, -1).wait_send()


def exchange(loc, sizes, collective_id):
    rows, cols, auxs = sizes
    count = cols * auxs
    height, width = loc.shape
    pieces = max(1, 16 // rows)
    shape = slab_shape(count, height, width)
    hops = cols - 1 + cols * (auxs - 1)
    any_space = pl.BlockSpec(memory_space=pl.ANY)
    _, mine, other = pl.pallas_call(
        functools.partial(exchange_kernel, rows, cols, auxs, pieces),
        out_shape=(
            jax.ShapeDtypeStruct((rows, height, width), loc.dtype),
            jax.ShapeDtypeStruct(shape, loc.dtype),
            jax.ShapeDtypeStruct(shape, loc.dtype),
        ),
        in_specs=[any_space],
        out_specs=(any_space, any_space, any_space),
        scratch_shapes=[
            pltpu.SemaphoreType.DMA((2, rows, pieces)),
            pltpu.SemaphoreType.DMA((rows, pieces)),
            pltpu.SemaphoreType.DMA((rows, pieces)),
            pltpu.SemaphoreType.DMA((count, pieces)),
            pltpu.SemaphoreType.DMA((hops,)),
            pltpu.SemaphoreType.DMA((count,)),
            pltpu.SemaphoreType.DMA((1 + pieces,)),
        ],
        compiler_params=pltpu.CompilerParams(
            collective_id=collective_id, has_side_effects=True
        ),
        name="exchange%d" % collective_id,
    )(loc)
    return whole(mine), whole(other)


def reduce_kernel(
    rows, cols, auxs, pieces, part, fock, total, diag, landed,
    psend, precv, dsend, drecv, lsem,
):
    row, col, aux = lax.axis_index("row"), lax.axis_index("col"), lax.axis_index("aux")
    count = cols * auxs
    me = col * auxs + aux
    height, width = total.shape
    size = height // pieces
    meet(row, col, aux, rows, cols, auxs)

    def p_copy(index, slot):
        return pltpu.make_async_remote_copy(
            src_ref=slab(part, index, width, 0, height),
            dst_ref=landed.at[slot],
            send_sem=psend.at[index],
            recv_sem=precv.at[slot],
            device_id={"col": index // auxs, "aux": lax.rem(index, auxs)},
            device_id_type=MESH,
        )

    def d_copy(p, step, own):
        piece = pl.ds(p * size, size)
        return pltpu.make_async_remote_copy(
            src_ref=fock.at[piece] if own else diag.at[piece],
            dst_ref=diag.at[piece],
            send_sem=dsend.at[(1 - step) // 2, p],
            recv_sem=drecv.at[p],
            device_id={"row": row + step},
            device_id_type=MESH,
        )

    for step in range(1, count):
        p_copy(lax.rem(me + step, count), me).start()
    own_part = pltpu.make_async_copy(
        slab(part, me, width, 0, height), landed.at[me], lsem.at[0]
    )
    own_part.start()
    own_diag = pltpu.make_async_copy(fock, diag, lsem.at[1])

    @pl.when(row == me)
    def _():
        own_diag.start()

    up, down = row < rows - 1, row > 0
    for p in range(pieces):
        @pl.when((row == me) & up)
        def _(p=p):
            d_copy(p, 1, True).start()

        @pl.when((row == me) & down)
        def _(p=p):
            d_copy(p, -1, True).start()

        @pl.when(row > me)
        def _(p=p):
            d_copy(p, 1, False).wait_recv()

            @pl.when(up)
            def _():
                d_copy(p, 1, False).start()

        @pl.when(row < me)
        def _(p=p):
            d_copy(p, -1, False).wait_recv()

            @pl.when(down)
            def _():
                d_copy(p, -1, False).start()

    own_part.wait()
    for step in range(1, count):
        p_copy(me, lax.rem(me + step, count)).wait_recv()

    tile = 256

    @pl.loop(0, height // tile)
    def _(i):
        at = pl.ds(pl.multiple_of(i * tile, tile), tile)
        acc = landed[0, at, :].astype(jnp.float32)
        for index in range(1, count):
            acc = acc + landed[index, at, :].astype(jnp.float32)
        total[at, :] = acc.astype(total.dtype)

    for step in range(1, count):
        p_copy(lax.rem(me + step, count), me).wait_send()

    @pl.when(row == me)
    def _():
        own_diag.wait()

    for p in range(pieces):
        @pl.when(up & (row >= me))
        def _(p=p):
            d_copy(p, 1, False).wait_send()

        @pl.when(down & (row <= me))
        def _(p=p):
            d_copy(p, -1, False).wait_send()


def reduce_rows(part, fock, sizes, collective_id):
    rows, cols, auxs = sizes
    count = cols * auxs
    height, virt = fock.shape
    width = part.shape[1] // count
    pieces = 4
    if width % LANES:
        part = part.reshape(height, count, width).transpose(1, 0, 2)
    any_space = pl.BlockSpec(memory_space=pl.ANY)
    return pl.pallas_call(
        functools.partial(reduce_kernel, rows, cols, auxs, pieces),
        out_shape=(
            jax.ShapeDtypeStruct((height, width), part.dtype),
            jax.ShapeDtypeStruct((height, virt), fock.dtype),
        ),
        in_specs=[any_space, any_space],
        out_specs=(pl.BlockSpec(memory_space=pltpu.VMEM), any_space),
        scratch_shapes=[
            pltpu.VMEM((count, height, width), part.dtype),
            pltpu.SemaphoreType.DMA((count,)),
            pltpu.SemaphoreType.DMA((count,)),
            pltpu.SemaphoreType.DMA((2, pieces)),
            pltpu.SemaphoreType.DMA((pieces,)),
            pltpu.SemaphoreType.DMA((2,)),
        ],
        compiler_params=pltpu.CompilerParams(
            collective_id=collective_id, has_side_effects=True, vmem_limit_bytes=VMEM_BYTES
        ),
        name="reduce%d" % collective_id,
    )(part, fock)


def update_kernel(
    virt, tile, t_ref, g_row, b_row, f_row, e_row, g_col, b_col, f_col, e_col, out
):
    high, across = t_ref.shape
    contract = (((1,), (1,)), ((), ()))

    @pl.loop(0, across // tile)
    def _(j):
        base = pl.multiple_of(j * tile, tile)
        at = pl.ds(base, tile)
        acc = lax.dot_general(
            g_row[...], b_col[at, :], contract, preferred_element_type=jnp.float32
        )
        acc = acc + lax.dot_general(
            b_row[...], g_col[at, :], contract, preferred_element_type=jnp.float32
        )
        right = [
            jnp.dot(
                t_ref[:, pl.ds(pl.multiple_of(base + k * virt, virt), virt)],
                f_col[pl.ds(pl.multiple_of(base + k * virt, virt), virt), :],
                preferred_element_type=jnp.float32,
            )
            for k in range(tile // virt)
        ]
        left = [
            lax.dot_general(
                f_row[k * virt:(k + 1) * virt, :],
                t_ref[k * virt:(k + 1) * virt, at],
                (((0,), (0,)), ((), ())),
                preferred_element_type=jnp.float32,
            )
            for k in range(high // virt)
        ]
        acc = acc + jnp.concatenate(right, axis=1) + jnp.concatenate(left, axis=0)
        delta = e_row[...] + e_col[:, at]
        out[:, at] = (t_ref[:, at].astype(jnp.float32) - acc / delta).astype(out.dtype)


def update(amplitudes, g_rows, b_rows, fock, e_rows, g_cols, b_cols, diag, e_cols):
    high, across = amplitudes.shape
    virt = fock.shape[1]
    aux = b_rows.shape[1]
    row_tile, col_tile = min(ROW_TILE, high), min(COL_TILE, across)
    by_row = lambda i: (i, 0)
    fixed = lambda i: (0, 0)
    return pl.pallas_call(
        functools.partial(update_kernel, virt, col_tile),
        out_shape=jax.ShapeDtypeStruct(amplitudes.shape, amplitudes.dtype),
        grid=(high // row_tile,),
        in_specs=[
            pl.BlockSpec((row_tile, across), by_row),
            pl.BlockSpec((row_tile, aux), by_row),
            pl.BlockSpec((row_tile, aux), by_row),
            pl.BlockSpec((row_tile, virt), by_row),
            pl.BlockSpec((row_tile, 1), by_row),
            pl.BlockSpec((across, aux), fixed),
            pl.BlockSpec((across, aux), fixed),
            pl.BlockSpec((across, virt), fixed),
            pl.BlockSpec((1, across), fixed),
        ],
        out_specs=pl.BlockSpec((row_tile, across), by_row),
        compiler_params=pltpu.CompilerParams(vmem_limit_bytes=VMEM_BYTES),
        name="update",
    )(amplitudes, g_rows, b_rows, fock, e_rows, g_cols, b_cols, diag, e_cols)


def body(sizes, amplitudes, b_factors, fock_blocks, occ_index, virt_index, eps_occ, eps_virt):
    height, across = amplitudes.shape
    b_rows, b_cols = exchange(b_factors, sizes, 0)
    part = jnp.dot(amplitudes, b_cols, preferred_element_type=jnp.float32)
    g_own, diag = reduce_rows(part.astype(jnp.bfloat16), fock_blocks, sizes, 1)
    g_rows, g_cols = exchange(g_own, sizes, 2)

    def energy(start, size):
        return pair_energy(
            lax.dynamic_slice_in_dim(occ_index, start, size),
            lax.dynamic_slice_in_dim(virt_index, start, size),
            eps_occ,
            eps_virt,
        )

    e_rows = energy(lax.axis_index("row") * height, height)
    e_cols = energy(lax.axis_index(("col", "aux")) * across, across)
    return update(
        amplitudes, g_rows, b_rows, fock_blocks, e_rows[:, None],
        g_cols, b_cols, diag, e_cols[None, :],
    )


def solution(mesh):
    in_specs = (
        P(("groups", "row"), ("col", "aux")),
        P(("groups", "row"), ("col", "aux")),
        P(("groups", "row"), None),
        P("groups"),
        P("groups"),
        P("groups"),
        P("groups"),
    )
    out_specs = P(("groups", "row"), ("col", "aux"))
    sizes = (mesh.shape["row"], mesh.shape["col"], mesh.shape["aux"])
    return jax.shard_map(
        functools.partial(body, sizes),
        mesh=mesh, in_specs=in_specs, out_specs=out_specs, check_vma=False,
    )
```

time: 767 us -> 339 us (0.44)
  waiting for transfers between devices: 440 us -> 0 us
  Pallas kernels: 0 us -> 307 us
  matrix products: 224 us -> 24.5 us
  local copies, waits for them, and re-layouts: 67.7 us -> 2.76 us
  between operations: 13.2 us -> 0.04 us
  other arithmetic: 13.8 us -> 4.89 us
    pallas_call x0 -> x4, Pallas kernels: none -> 307 us  [the longest x2 183 us: exchange(): pl.pallas_call(functools.partial(exchange_kernel, rows, cols, auxs, piece...]
    dot_general x5 -> x1, matrix products: 224 us -> 24.5 us  [body(): part = jnp.dot(amplitudes, b_cols, preferred_element_type=jnp.float32)]
    psum x2 -> x0, waiting for transfers between devices: 185 us -> none  [spread(): return lax.psum(jnp.where(mine, shard, jnp.zeros_like(shard)), axis)]
    reduce_scatter x1 -> x0, waiting for transfers between devices: 137 us -> none  [body(): lax.psum_scatter(lax.dot_general(amplitudes, b_rows, (((0,), (0,)), ((),...]
    all_gather x2 -> x0, waiting for transfers between devices: 118 us -> none  [the longest x1 80.7 us: body(): g_cols = lax.all_gather(g_slice, 'row', axis=0, tiled=True)]
    reshape x1 -> x0, local copies, waits for them, and re-layouts: 66.1 us -> none  [body(): right.reshape(rows_blk, rows_blk)]
    select_n x2 -> x0, other arithmetic: 8.13 us -> none  [spread(): return lax.psum(jnp.where(mine, shard, jnp.zeros_like(shard)), axis)]
  transfers between devices with their start and end apart: 5 -> 0, of which waited for: 4 -> 0; matrix products, arithmetic and copies ran while one was open for 21% -> 0% of each run, Pallas kernels for 0% -> 0%
where the time goes in v1:
time: 339 us
  Pallas kernels  307 us (91%)
  matrix products  24.5 us (7%)
  other arithmetic  4.89 us (1%)
    pallas_call x2, Pallas kernels, exchange(): pl.pallas_call(functools.partial(exchange_kernel, rows, cols, auxs, piece...  183 us
    pallas_call x1, Pallas kernels, update(): pl.pallas_call(functools.partial(update_kernel, virt, col_tile), out_shap...  74.6 us
    pallas_call x1, Pallas kernels, reduce_rows(): pl.pallas_call(functools.partial(reduce_kernel, rows, cols, auxs, pieces)...  48.6 us
    dot_general x1, matrix products, body(): part = jnp.dot(amplitudes, b_cols, preferred_element_type=jnp.float32)  24.5 us

profile of v1, /device:TPU:24, one launch (start us, length us, event | category | flops | bytes accessed | tf_op | source)
XLA Modules:
  0.0 338.7 jit_solution(7565108892928758184)
XLA Ops:
  0.0 0.8 fusion
  0.8 1.0 select_reduce_fusion.2
  1.8 3.2 select_reduce_fusion
  5.1 0.6 sub.28
  5.7 2.0 copy.9.e_row
  7.7 88.1 %exchange0.1 = (bf16[4,4096,128]{2,1,0:T(8,128)(2,1)}, bf16[4096,512]{1,0:T(8,128)(2,1)}, bf16[4096,512]{1,0:T(8,128)(2,1)}) custom-call(bf16[4096,128]{1,0:T(8,128)(2,1)} %loc.1), custom_call_target="tpu_custom_call" | custom-call | tf_op jit(solution)/shard_map/exchange0/pallas_call | solution.py:224
  95.8 24.5 %convolution_convert_fusion.part = bf16[4096,512]{1,0:T(8,128)(2,1)} fusion(bf16[4096,4096]{1,0:T(8,128)(2,1)} %t_ref.1, bf16[4096,512]{1,0:T(8,128)(2,1)} %get-tuple-element.11.b_col), kind=kOutput, calls=%fused_computation | convolution fusion | flops 17181966336 | bytes 41943040 | tf_op jit(solution)/shard_map/dot_general | solution.py:452
  120.2 48.6 %reduce1.1 = (bf16[4096,128]{1,0:T(8,128)(2,1)}, bf16[4096,256]{1,0:T(8,128)(2,1)}) custom-call(bf16[4096,512]{1,0:T(8,128)(2,1)} %convolution_convert_fusion.part, bf16[4096,256]{1,0:T(8,128)(2,1)} %f_row.1), custom_call_target="tpu_custom_call" | custom-call | tf_op jit(solution)/shard_map/reduce1/pallas_call | solution.py:360
  168.9 95.3 %exchange2.1 = (bf16[4,4096,128]{2,1,0:T(8,128)(2,1)}, bf16[4096,512]{1,0:T(8,128)(2,1)}, bf16[4096,512]{1,0:T(8,128)(2,1)}) custom-call(bf16[4096,128]{1,0:T(8,128)(2,1)} %get-tuple-element.12.loc), custom_call_target="tpu_custom_call" | custom-call | tf_op jit(solution)/shard_map/exchange2/pallas_call | solution.py:224
  264.1 74.6 %update.1 = bf16[4096,4096]{1,0:T(8,128)(2,1)} custom-call(bf16[4096,4096]{1,0:T(8,128)(2,1)} %t_ref.1, bf16[4096,512]{1,0:T(8,128)(2,1)} %get-tuple-element.13.g_row, bf16[4096,512]{1,0:T(8,128)(2,1)} %get-tuple-element.14.b_row, bf16[4096,256]{1,0:T(8,128)(2,1)} %f_row.1, f32[4096,1]{1,0:T(8,128)} %copy.9.e_row, ...), custom_call_target="tpu_custom_call" | custom-call | tf_op jit(solution)/shard_map/update/pallas_call | solution.py:428
  (1 shorter events, 0.0 us)

commit v2 on v1

--- a/solution.py
+++ b/solution.py
@@ -10,7 +10,7 @@
 MESH = pl.DeviceIdType.MESH
 LANES = 128
 ROW_TILE = 512
-COL_TILE = 512
+COL_TILE = 1024
 VMEM_BYTES = 60 * 1024 * 1024
 
 
@@ -248,22 +248,30 @@
 
 
 def reduce_kernel(
-    rows, cols, auxs, pieces, part, fock, total, diag, landed,
-    psend, precv, dsend, drecv, lsem,
+    rows, cols, auxs, groups, amps, b_col, fock, total, diag, part, landed, held,
+    psend, precv, dsend, drecv, lsem, tsem,
 ):
     row, col, aux = lax.axis_index("row"), lax.axis_index("col"), lax.axis_index("aux")
     count = cols * auxs
     me = col * auxs + aux
     height, width = total.shape
-    size = height // pieces
+    size = height // groups
+    tile = min(size, 256)
+
+    def fetch(g):
+        return pltpu.make_async_copy(
+            amps.at[pl.ds(g * size, size)], held.at[g % 2], tsem.at[g % 2]
+        )
+
+    fetch(0).start()
     meet(row, col, aux, rows, cols, auxs)
 
-    def p_copy(index, slot):
+    def p_copy(g, index, slot):
         return pltpu.make_async_remote_copy(
-            src_ref=slab(part, index, width, 0, height),
-            dst_ref=landed.at[slot],
-            send_sem=psend.at[index],
-            recv_sem=precv.at[slot],
+            src_ref=part.at[index, pl.ds(g * size, size)],
+            dst_ref=landed.at[slot, pl.ds(g * size, size)],
+            send_sem=psend.at[g, index],
+            recv_sem=precv.at[g, slot],
             device_id={"col": index // auxs, "aux": lax.rem(index, auxs)},
             device_id_type=MESH,
         )
@@ -279,20 +287,14 @@
             device_id_type=MESH,
         )
 
-    for step in range(1, count):
-        p_copy(lax.rem(me + step, count), me).start()
-    own_part = pltpu.make_async_copy(
-        slab(part, me, width, 0, height), landed.at[me], lsem.at[0]
-    )
-    own_part.start()
-    own_diag = pltpu.make_async_copy(fock, diag, lsem.at[1])
+    own_diag = pltpu.make_async_copy(fock, diag, lsem.at[0])
+    up, down = row < rows - 1, row > 0
 
     @pl.when(row == me)
     def _():
         own_diag.start()
 
-    up, down = row < rows - 1, row > 0
-    for p in range(pieces):
+    for p in range(groups):
         @pl.when((row == me) & up)
         def _(p=p):
             d_copy(p, 1, True).start()
@@ -301,8 +303,9 @@
         def _(p=p):
             d_copy(p, -1, True).start()
 
+    def forward(p):
         @pl.when(row > me)
-        def _(p=p):
+        def _():
             d_copy(p, 1, False).wait_recv()
 
             @pl.when(up)
@@ -310,35 +313,58 @@
                 d_copy(p, 1, False).start()
 
         @pl.when(row < me)
-        def _(p=p):
+        def _():
             d_copy(p, -1, False).wait_recv()
 
             @pl.when(down)
             def _():
                 d_copy(p, -1, False).start()
 
-    own_part.wait()
-    for step in range(1, count):
-        p_copy(me, lax.rem(me + step, count)).wait_recv()
-
-    tile = 256
-
-    @pl.loop(0, height // tile)
-    def _(i):
-        at = pl.ds(pl.multiple_of(i * tile, tile), tile)
-        acc = landed[0, at, :].astype(jnp.float32)
-        for index in range(1, count):
-            acc = acc + landed[index, at, :].astype(jnp.float32)
-        total[at, :] = acc.astype(total.dtype)
-
-    for step in range(1, count):
-        p_copy(lax.rem(me + step, count), me).wait_send()
+    ahead = max(groups // 2, 1)
+    for g in range(groups):
+        if g + 1 < groups:
+            fetch(g + 1).start()
+        fetch(g).wait()
+
+        @pl.loop(0, size // tile)
+        def _(i, g=g):
+            at = pl.ds(pl.multiple_of(i * tile, tile), tile)
+            to = pl.ds(pl.multiple_of(g * size + i * tile, tile), tile)
+            product = jnp.dot(
+                held[g % 2, at, :], b_col[...], preferred_element_type=jnp.float32
+            ).astype(part.dtype)
+            for index in range(count):
+                part[index, to, :] = product[:, index * width:(index + 1) * width]
+
+        for step in range(1, count):
+            p_copy(g, lax.rem(me + step, count), me).start()
+        if g >= ahead:
+            forward(g - ahead)
+    for p in range(groups - ahead, groups):
+        forward(p)
+
+    for g in range(groups):
+        for step in range(1, count):
+            p_copy(g, me, lax.rem(me + step, count)).wait_recv()
+
+        @pl.loop(0, size // tile)
+        def _(i, g=g):
+            at = pl.ds(pl.multiple_of(g * size + i * tile, tile), tile)
+            acc = part[me, at, :].astype(jnp.float32)
+            for step in range(1, count):
+                index = lax.rem(me + step, count)
+                acc = acc + landed[index, at, :].astype(jnp.float32)
+            total[at, :] = acc.astype(total.dtype)
+
+    for g in range(groups):
+        for step in range(1, count):
+            p_copy(g, lax.rem(me + step, count), me).wait_send()
 
     @pl.when(row == me)
     def _():
         own_diag.wait()
 
-    for p in range(pieces):
+    for p in range(groups):
         @pl.when(up & (row >= me))
         def _(p=p):
             d_copy(p, 1, False).wait_send()
@@ -348,36 +374,39 @@
             d_copy(p, -1, False).wait_send()
 
 
-def reduce_rows(part, fock, sizes, collective_id):
+def reduce_rows(amps, b_cols, fock, sizes, collective_id):
     rows, cols, auxs = sizes
     count = cols * auxs
     height, virt = fock.shape
-    width = part.shape[1] // count
-    pieces = 4
-    if width % LANES:
-        part = part.reshape(height, count, width).transpose(1, 0, 2)
+    across = amps.shape[1]
+    width = b_cols.shape[1] // count
+    groups = max(1, height // 512)
     any_space = pl.BlockSpec(memory_space=pl.ANY)
+    in_vmem = pl.BlockSpec(memory_space=pltpu.VMEM)
     return pl.pallas_call(
-        functools.partial(reduce_kernel, rows, cols, auxs, pieces),
+        functools.partial(reduce_kernel, rows, cols, auxs, groups),
         out_shape=(
-            jax.ShapeDtypeStruct((height, width), part.dtype),
+            jax.ShapeDtypeStruct((height, width), amps.dtype),
             jax.ShapeDtypeStruct((height, virt), fock.dtype),
         ),
-        in_specs=[any_space, any_space],
-        out_specs=(pl.BlockSpec(memory_space=pltpu.VMEM), any_space),
+        in_specs=[any_space, in_vmem, any_space],
+        out_specs=(in_vmem, any_space),
         scratch_shapes=[
-            pltpu.VMEM((count, height, width), part.dtype),
-            pltpu.SemaphoreType.DMA((count,)),
-            pltpu.SemaphoreType.DMA((count,)),
-            pltpu.SemaphoreType.DMA((2, pieces)),
-            pltpu.SemaphoreType.DMA((pieces,)),
+            pltpu.VMEM((count, height, width), amps.dtype),
+            pltpu.VMEM((count, height, width), amps.dtype),
+            pltpu.VMEM((2, height // groups, across), amps.dtype),
+            pltpu.SemaphoreType.DMA((groups, count)),
+            pltpu.SemaphoreType.DMA((groups, count)),
+            pltpu.SemaphoreType.DMA((2, groups)),
+            pltpu.SemaphoreType.DMA((groups,)),
+            pltpu.SemaphoreType.DMA((1,)),
             pltpu.SemaphoreType.DMA((2,)),
         ],
         compiler_params=pltpu.CompilerParams(
             collective_id=collective_id, has_side_effects=True, vmem_limit_bytes=VMEM_BYTES
         ),
         name="reduce%d" % collective_id,
-    )(part, fock)
+    )(amps, b_cols, fock)
 
 
 def update_kernel(
@@ -449,8 +478,7 @@
 def body(sizes, amplitudes, b_factors, fock_blocks, occ_index, virt_index, eps_occ, eps_virt):
     height, across = amplitudes.shape
     b_rows, b_cols = exchange(b_factors, sizes, 0)
-    part = jnp.dot(amplitudes, b_cols, preferred_element_type=jnp.float32)
-    g_own, diag = reduce_rows(part.astype(jnp.bfloat16), fock_blocks, sizes, 1)
+    g_own, diag = reduce_rows(amplitudes, b_cols, fock_blocks, sizes, 1)
     g_rows, g_cols = exchange(g_own, sizes, 2)
 
     def energy(start, size):

time: 339 us -> 313 us (0.923)
  matrix products: 24.5 us -> 0 us
    dot_general x1 -> x0, matrix products: 24.5 us -> none  [body(): part = jnp.dot(amplitudes, b_cols, preferred_element_type=jnp.float32)]
    pallas_call x1, Pallas kernels: 74.6 us -> 69.9 us  [update(): pl.pallas_call(functools.partial(update_kernel, virt, col_tile), out_shap...]
    pallas_call x1, Pallas kernels: 48.6 us -> 52.4 us  [reduce_rows(): pl.pallas_call(functools.partial(reduce_kernel, rows, cols, auxs, groups)...]
where the time goes in v2:
time: 313 us; the launch traced here: 312 us
  Pallas kernels  305 us (97%)
  other arithmetic  4.89 us (2%)
    pallas_call x2, Pallas kernels, exchange(): pl.pallas_call(functools.partial(exchange_kernel, rows, cols, auxs, piece...  182 us
    pallas_call x1, Pallas kernels, update(): pl.pallas_call(functools.partial(update_kernel, virt, col_tile), out_shap...  69.9 us
    pallas_call x1, Pallas kernels, reduce_rows(): pl.pallas_call(functools.partial(reduce_kernel, rows, cols, auxs, groups)...  52.4 us

profile of v2, /device:TPU:24, one launch (start us, length us, event | category | flops | bytes accessed | tf_op | source)
XLA Modules:
  0.0 312.5 jit_solution(9311178784887997767)
XLA Ops:
  0.0 0.8 fusion
  0.8 1.0 select_reduce_fusion.2
  1.8 3.2 %select_reduce_fusion = (f32[4096]{0:T(1024)S(1)}, f32[4096]{0:T(1024)S(1)}) fusion(s32[4096]{0:T(1024)S(1)} %get-tuple-element.25, f32[256]{0:T(256)} %param.13, s32[4096]{0:T(1024)S(1)} %get-tuple-element.26), kind=kLoop, calls=%fused_computation | loop fusion | flops 6283264 | bytes 66560 | tf_op jit(solution)/shard_map/reduce_sum | solution.py:20
  5.1 0.6 sub.28
  5.7 2.0 copy.9.e_row
  7.7 88.1 %exchange0.1 = (bf16[4,4096,128]{2,1,0:T(8,128)(2,1)}, bf16[4096,512]{1,0:T(8,128)(2,1)}, bf16[4096,512]{1,0:T(8,128)(2,1)}) custom-call(bf16[4096,128]{1,0:T(8,128)(2,1)} %loc.1), custom_call_target="tpu_custom_call" | custom-call | tf_op jit(solution)/shard_map/exchange0/pallas_call | solution.py:224
  95.8 52.4 %reduce1.1 = (bf16[4096,128]{1,0:T(8,128)(2,1)}, bf16[4096,256]{1,0:T(8,128)(2,1)}) custom-call(bf16[4096,4096]{1,0:T(8,128)(2,1)} %t_ref.1, bf16[4096,512]{1,0:T(8,128)(2,1)} %get-tuple-element.11.b_col, bf16[4096,256]{1,0:T(8,128)(2,1)} %f_row.1), custom_call_target="tpu_custom_call" | custom-call | tf_op jit(solution)/shard_map/reduce1/pallas_call | solution.py:386
  148.2 94.3 %exchange2.1 = (bf16[4,4096,128]{2,1,0:T(8,128)(2,1)}, bf16[4096,512]{1,0:T(8,128)(2,1)}, bf16[4096,512]{1,0:T(8,128)(2,1)}) custom-call(bf16[4096,128]{1,0:T(8,128)(2,1)} %get-tuple-element.12.loc), custom_call_target="tpu_custom_call" | custom-call | tf_op jit(solution)/shard_map/exchange2/pallas_call | solution.py:224
  242.5 69.9 %update.1 = bf16[4096,4096]{1,0:T(8,128)(2,1)} custom-call(bf16[4096,4096]{1,0:T(8,128)(2,1)} %t_ref.1, bf16[4096,512]{1,0:T(8,128)(2,1)} %get-tuple-element.13.g_row, bf16[4096,512]{1,0:T(8,128)(2,1)} %get-tuple-element.14.b_row, bf16[4096,256]{1,0:T(8,128)(2,1)} %f_row.1, f32[4096,1]{1,0:T(8,128)} %copy.9.e_row, ...), custom_call_target="tpu_custom_call" | custom-call | tf_op jit(solution)/shard_map/update/pallas_call | solution.py:457
  (1 shorter events, 0.0 us)

commit v3 on v2

--- a/solution.py
+++ b/solution.py
@@ -175,7 +175,7 @@
                     z_copy(k, p, -1).start()
 
                 dispatch(k, p)
-        if s == 1:
+        if s == max(1, rows - 2):
             for index, copy in second[auxs - 1:]:
                 r_copy(index, col, aux, 0, False).wait_recv()
                 copy.start()
@@ -217,7 +217,7 @@
     rows, cols, auxs = sizes
     count = cols * auxs
     height, width = loc.shape
-    pieces = max(1, 16 // rows)
+    pieces = max(1, 32 // rows)
     shape = slab_shape(count, height, width)
     hops = cols - 1 + cols * (auxs - 1)
     any_space = pl.BlockSpec(memory_space=pl.ANY)

time: 313 us -> 310 us (level)
  no operation moved by 1% of the time
where the time goes in v3:
time: 310 us
  Pallas kernels  302 us (97%)
  other arithmetic  4.89 us (2%)
    pallas_call x2, Pallas kernels, exchange(): pl.pallas_call(functools.partial(exchange_kernel, rows, cols, auxs, piece...  180 us
    pallas_call x1, Pallas kernels, update(): pl.pallas_call(functools.partial(update_kernel, virt, col_tile), out_shap...  69.9 us
    pallas_call x1, Pallas kernels, reduce_rows(): pl.pallas_call(functools.partial(reduce_kernel, rows, cols, auxs, groups)...  52.4 us

profile of v3, /device:TPU:24, one launch (start us, length us, event | category | flops | bytes accessed | tf_op | source)
XLA Modules:
  0.0 309.8 jit_solution(9110028003244735774)
XLA Ops:
  0.0 0.8 fusion
  0.8 1.0 select_reduce_fusion.2
  1.8 3.2 %select_reduce_fusion = (f32[4096]{0:T(1024)S(1)}, f32[4096]{0:T(1024)S(1)}) fusion(s32[4096]{0:T(1024)S(1)} %get-tuple-element.25, f32[256]{0:T(256)} %param.13, s32[4096]{0:T(1024)S(1)} %get-tuple-element.26), kind=kLoop, calls=%fused_computation | loop fusion | flops 6283264 | bytes 66560 | tf_op jit(solution)/shard_map/reduce_sum | solution.py:20
  5.1 0.6 sub.28
  5.7 2.0 copy.9.e_row
  7.7 86.1 %exchange0.1 = (bf16[4,4096,128]{2,1,0:T(8,128)(2,1)}, bf16[4096,512]{1,0:T(8,128)(2,1)}, bf16[4096,512]{1,0:T(8,128)(2,1)}) custom-call(bf16[4096,128]{1,0:T(8,128)(2,1)} %loc.1), custom_call_target="tpu_custom_call" | custom-call | tf_op jit(solution)/shard_map/exchange0/pallas_call | solution.py:224
  93.8 52.4 %reduce1.1 = (bf16[4096,128]{1,0:T(8,128)(2,1)}, bf16[4096,256]{1,0:T(8,128)(2,1)}) custom-call(bf16[4096,4096]{1,0:T(8,128)(2,1)} %t_ref.1, bf16[4096,512]{1,0:T(8,128)(2,1)} %get-tuple-element.11.b_col, bf16[4096,256]{1,0:T(8,128)(2,1)} %f_row.1), custom_call_target="tpu_custom_call" | custom-call | tf_op jit(solution)/shard_map/reduce1/pallas_call | solution.py:386
  146.2 93.7 %exchange2.1 = (bf16[4,4096,128]{2,1,0:T(8,128)(2,1)}, bf16[4096,512]{1,0:T(8,128)(2,1)}, bf16[4096,512]{1,0:T(8,128)(2,1)}) custom-call(bf16[4096,128]{1,0:T(8,128)(2,1)} %get-tuple-element.12.loc), custom_call_target="tpu_custom_call" | custom-call | tf_op jit(solution)/shard_map/exchange2/pallas_call | solution.py:224
  239.9 69.9 %update.1 = bf16[4096,4096]{1,0:T(8,128)(2,1)} custom-call(bf16[4096,4096]{1,0:T(8,128)(2,1)} %t_ref.1, bf16[4096,512]{1,0:T(8,128)(2,1)} %get-tuple-element.13.g_row, bf16[4096,512]{1,0:T(8,128)(2,1)} %get-tuple-element.14.b_row, bf16[4096,256]{1,0:T(8,128)(2,1)} %f_row.1, f32[4096,1]{1,0:T(8,128)} %copy.9.e_row, ...), custom_call_target="tpu_custom_call" | custom-call | tf_op jit(solution)/shard_map/update/pallas_call | solution.py:457
  (1 shorter events, 0.0 us)
